TPU v7x, 128 devices: a whole 4x4x4 slice. The times are simulated.
128 devices in a mesh: dp: 32 (over z, y_hi, x), tensor: 4 (over y_lo, core).
Axes of the slice: x: 4, y: 4 (y_hi: 2, y_lo: 2; y = y_hi * 2 + y_lo), z: 4, core: 2. Of those that a mesh axis runs over, the one named last changes fastest.
Arguments:
- tokens: bfloat16 [32, 4, 128, 2048], P('dp', 'tensor'), may hold values from -6 to 6
- doc_ids: int32 [32, 4, 128], P('dp'), may hold values from 0 to 3, never falling along the last dimension, each value on 1 to 64 neighbouring positions
- attn_gain: float32 [2048], P(('dp', 'tensor')), may hold values from 0.5 to 1.5
- forget_floor: float32 [2048], P(('dp', 'tensor')), may hold values from 0.5 to 0.98
- w_query: bfloat16 [2048, 2048], P('dp', 'tensor'), may hold values from -0.125 to 0.125
- w_forget: bfloat16 [2048, 2048], P('dp', 'tensor'), may hold values from -0.125 to 0.125
- w_value: bfloat16 [2048, 2048], P('dp', 'tensor'), may hold values from -0.125 to 0.125
- w_outgate: bfloat16 [2048, 2048], P('dp', 'tensor'), may hold values from -0.125 to 0.125
- w_output: bfloat16 [2048, 2048], P('tensor', 'dp'), may hold values from -0.125 to 0.125
- mlp_gain: float32 [2048], P(('dp', 'tensor')), may hold values from 0.5 to 1.5
- w_gate: bfloat16 [2048, 5632], P('dp', 'tensor'), may hold values from -0.125 to 0.125
- w_up: bfloat16 [2048, 5632], P('dp', 'tensor'), may hold values from -0.125 to 0.125
- w_down: bfloat16 [5632, 2048], P('tensor', 'dp'), may hold values from -0.078125 to 0.078125
- cotangent: bfloat16 [32, 4, 128, 2048], P('dp', 'tensor'), may hold values from -6 to 6
Outputs:
- layer_out: bfloat16 [32, 4, 128, 2048], P('dp', 'tensor')
- grad_tokens: float32 [32, 4, 128, 2048], P('dp', 'tensor')
- grad_attn_gain: float32 [2048], P(('dp', 'tensor'))
- grad_floor: float32 [2048], P(('dp', 'tensor'))
- grad_query: float32 [2048, 2048], P('dp', 'tensor')
- grad_forget: float32 [2048, 2048], P('dp', 'tensor')
- grad_value: float32 [2048, 2048], P('dp', 'tensor')
- grad_outgate: float32 [2048, 2048], P('dp', 'tensor')
- grad_output: float32 [2048, 2048], P('tensor', 'dp')
- grad_mlp_gain: float32 [2048], P(('dp', 'tensor'))
- grad_gate: float32 [2048, 5632], P('dp', 'tensor')
- grad_up: float32 [2048, 5632], P('dp', 'tensor')
- grad_down: float32 [5632, 2048], P('tensor', 'dp')
Inputs may be any that keep to these rules, and one draw needn't show every extreme that they name: `doc_ids`: within each row of 128 tokens the sequence numbers never fall; each sequence has 1 to 64 tokens, and the longest has exactly 64.
All inputs are finite; a program needn't handle non-finite values.
Results may differ from a plain program's by a relative error of at most 0.025.
Values may be sent and summed in bfloat16 or wider, within the bound.
No kernel may reach another device: no remote copies, remote signals or barrier semaphores. Data moves between devices by JAX's collectives and lax.ppermute only.
A program may use at most 192 MiB of HBM per device.

v0:
```python
import jax
import jax.numpy as jnp
from jax import lax
from jax.sharding import PartitionSpec as P

HK = 128
HIGHEST = lax.Precision.HIGHEST
epsilon = 1e-06


def row_scale(values):
    return lax.rsqrt(jnp.mean(values * values, axis=-1, keepdims=True) + epsilon)


def silu_slope(values):
    sigmoid_val = jax.nn.sigmoid(values)
    return sigmoid_val * (1.0 + values * (1.0 - sigmoid_val))


def matmul_plain(left, right):
    return jnp.dot(left, right, preferred_element_type=jnp.float32)


def times_trans(left, right):
    return lax.dot_general(
        left, right, (((1,), (1,)), ((), ())), preferred_element_type=jnp.float32
    )


def trans_times(left, right):
    return lax.dot_general(
        left, right, (((0,), (0,)), ((), ())), preferred_element_type=jnp.float32
    )


def recurrence(query, forget_raw, value, floor_vec, doc_rows):
    length = query.shape[1]
    forget = floor_vec + (1.0 - floor_vec) * jax.nn.sigmoid(forget_raw)
    log_forget = jnp.log(forget)
    keyed = 1.0 - forget
    position = jnp.arange(length)
    same_doc = doc_rows[:, :, None] == doc_rows[:, None, :]
    causal = same_doc & (position[:, None] >= position[None, :])
    starts = jnp.concatenate(
        [jnp.zeros_like(doc_rows[:, :1], dtype=bool), doc_rows[:, 1:] == doc_rows[:, :-1]], axis=1
    )
    summing = (causal & starts[:, None, :]).astype(jnp.float32)
    running = jnp.einsum("rij,rjhk->rihk", summing, log_forget, precision=HIGHEST)
    query_t = query * jnp.exp(running)
    key_t = keyed * jnp.exp(-running)
    scores = jnp.einsum("rihk,rjhk->rhij", query_t, key_t, precision=HIGHEST)
    scores = jnp.where(causal[:, None], scores, 0.0)
    return jnp.einsum("rhij,rjhv->rihv", scores, value, precision=HIGHEST)


ON_CHIP = [(0, 1), (1, 0), (2, 3), (3, 2)]
ACROSS = [(0, 2), (2, 0), (1, 3), (3, 1)]
SLOT_XOR = (0, 2, 1, 3)


def row_gather(values):
    across = lax.ppermute(values, "tensor", ACROSS)
    pair = jnp.stack([values, across])
    other = lax.ppermute(pair, "tensor", ON_CHIP)
    return jnp.concatenate([pair, other]).reshape((-1,) + values.shape[1:])


def row_sum(values):
    blocks = values.reshape((4, -1) + values.shape[1:])
    got = lax.ppermute(blocks[2:], "tensor", ON_CHIP)
    mine = blocks[0] + got[0]
    theirs = blocks[1] + got[1]
    return mine + lax.ppermute(theirs, "tensor", ACROSS)


def spread_sum(values, axis, count):
    blocks = values.reshape((count, -1) + values.shape[1:])
    got = lax.all_to_all(blocks, axis, 0, 0, tiled=False)
    return got.astype(jnp.float32).sum(axis=0)


def small_gather(vectors):
    count = 128
    spread = jnp.broadcast_to(vectors[None], (count,) + vectors.shape)
    got = lax.all_to_all(spread, ("dp", "tensor"), 0, 0, tiled=False)
    return jnp.swapaxes(got, 0, 1).reshape(vectors.shape[0], -1)


def small_sum(vectors):
    count = 128
    blocks = vectors.reshape(vectors.shape[0], count, -1)
    got = lax.all_to_all(jnp.swapaxes(blocks, 0, 1), ("dp", "tensor"), 0, 0, tiled=False)
    return got.sum(axis=0)


def shards(
    tokens,
    doc_ids,
    attn_gain,
    forget_floor,
    w_query,
    w_forget,
    w_value,
    w_outgate,
    w_output,
    mlp_gain,
    w_gate,
    w_up,
    w_down,
    cotangent,
):
    gains = small_gather(jnp.stack([attn_gain, forget_floor, mlp_gain]))
    attn_full, floor_full, mlp_full = (gains[0], gains[1], gains[2])
    part_index = lax.axis_index("tensor")
    local_width = w_query.shape[1]
    local_heads = local_width // HK
    hidden_width = w_gate.shape[1]
    floor_local = lax.dynamic_slice_in_dim(
        floor_full, part_index * local_width, local_width
    ).reshape(local_heads, HK)
    model_width = attn_full.shape[0]
    slot_rows = jnp.bitwise_xor(part_index, jnp.array(SLOT_XOR, jnp.int32))
    doc_all = jnp.take(doc_ids[0], slot_rows, axis=0)
    row_count = doc_all.shape[0]
    resid_in = tokens[0].reshape(-1, model_width).astype(jnp.float32)
    cot_local = cotangent[0].reshape(-1, model_width)
    attn_pack = jnp.concatenate([w_query, w_forget, w_value, w_outgate, w_output.T], axis=1)
    mlp_pack = jnp.concatenate([w_gate, w_up, w_down.T], axis=1)
    attn_all = lax.all_gather(attn_pack, "dp", axis=0, tiled=True)
    mlp_all = lax.all_gather(mlp_pack, "dp", axis=0, tiled=True)
    wq_all = attn_all[:, 0 * local_width : 1 * local_width]
    wf_all = attn_all[:, 1 * local_width : 2 * local_width]
    wv_all = attn_all[:, 2 * local_width : 3 * local_width]
    wg_all = attn_all[:, 3 * local_width : 4 * local_width]
    wo_t = attn_all[:, 4 * local_width : 5 * local_width]
    wgate_all = mlp_all[:, 0:hidden_width]
    wup_all = mlp_all[:, hidden_width : 2 * hidden_width]
    wdown_t = mlp_all[:, 2 * hidden_width : 3 * hidden_width]
    scale_one = row_scale(resid_in)
    normed = row_gather((resid_in * scale_one * attn_full).astype(jnp.bfloat16))
    query = matmul_plain(normed, wq_all)
    forget_raw = matmul_plain(normed, wf_all)
    value = matmul_plain(normed, wv_all)
    out_gate = matmul_plain(normed, wg_all)

    def mixer(query_in, forget_in, value_in, floor_in):

        def shaped(arr):
            return arr.reshape(row_count, -1, local_heads, HK)

        mixed_rows = recurrence(
            shaped(query_in), shaped(forget_in), shaped(value_in), floor_in, doc_all
        )
        return mixed_rows.reshape(query_in.shape[0], local_width)

    mixed, pullback = jax.vjp(mixer, query, forget_raw, value, floor_local)
    gate_act = jax.nn.silu(out_gate)
    gated = (mixed * gate_act).astype(jnp.bfloat16)
    branch = row_sum(times_trans(gated, wo_t))
    resid = resid_in + branch
    scale_two = row_scale(resid)
    normed2 = row_gather((resid * scale_two * mlp_full).astype(jnp.bfloat16))
    gate_proj = matmul_plain(normed2, wgate_all)
    up_proj = matmul_plain(normed2, wup_all)
    gate_silu = jax.nn.silu(gate_proj)
    hidden = (gate_silu * up_proj).astype(jnp.bfloat16)
    ffn_out = row_sum(times_trans(hidden, wdown_t))
    layer_out = (resid + ffn_out).astype(jnp.bfloat16).reshape(tokens.shape)
    cot_full = row_gather(cot_local)
    d_hidden = matmul_plain(cot_full, wdown_t)
    grad_down_t = trans_times(cot_full, hidden)
    d_gate = (d_hidden * up_proj * silu_slope(gate_proj)).astype(jnp.bfloat16)
    d_up = (d_hidden * gate_silu).astype(jnp.bfloat16)
    grad_gate = trans_times(normed2, d_gate)
    grad_up = trans_times(normed2, d_up)
    mlp_grads = jnp.concatenate(
        [
            grad_gate.astype(jnp.bfloat16),
            grad_up.astype(jnp.bfloat16),
            grad_down_t.astype(jnp.bfloat16),
        ],
        axis=1,
    )
    mlp_red = lax.psum_scatter(mlp_grads, "dp", scatter_dimension=0, tiled=True).astype(jnp.float32)
    d_normed2 = row_sum(times_trans(d_gate, wgate_all) + times_trans(d_up, wup_all))
    grad_mlp = jnp.sum(d_normed2 * resid * scale_two, axis=0)
    inner_two = jnp.mean(d_normed2 * mlp_full * resid, axis=-1, keepdims=True)
    d_resid = (
        cot_local.astype(jnp.float32)
        + d_normed2 * mlp_full * scale_two
        - resid * scale_two**3 * inner_two
    )
    d_branch = row_gather(d_resid.astype(jnp.bfloat16))
    d_gated = matmul_plain(d_branch, wo_t)
    grad_output_t = trans_times(d_branch, gated)
    d_mixed = d_gated * gate_act
    d_outgate = (d_gated * mixed * silu_slope(out_gate)).astype(jnp.bfloat16)
    d_query, d_forget, d_value, d_floor = pullback(d_mixed)
    d_query = d_query.astype(jnp.bfloat16)
    d_forget = d_forget.astype(jnp.bfloat16)
    d_value = d_value.astype(jnp.bfloat16)
    grad_query = trans_times(normed, d_query)
    grad_forget = trans_times(normed, d_forget)
    grad_value = trans_times(normed, d_value)
    grad_outgate = trans_times(normed, d_outgate)
    attn_grads = jnp.concatenate(
        [
            grad_query.astype(jnp.bfloat16),
            grad_forget.astype(jnp.bfloat16),
            grad_value.astype(jnp.bfloat16),
            grad_outgate.astype(jnp.bfloat16),
            grad_output_t.astype(jnp.bfloat16),
        ],
        axis=1,
    )
    attn_red = spread_sum(attn_grads, "dp", 32)
    d_normed = row_sum(
        times_trans(d_query, wq_all)
        + times_trans(d_forget, wf_all)
        + times_trans(d_value, wv_all)
        + times_trans(d_outgate, wg_all)
    )
    grad_attn = jnp.sum(d_normed * resid_in * scale_one, axis=0)
    inner_one = jnp.mean(d_normed * attn_full * resid_in, axis=-1, keepdims=True)
    grad_tokens = (
        d_resid + d_normed * attn_full * scale_one - resid_in * scale_one**3 * inner_one
    ).reshape(tokens.shape)
    floor_vector = lax.dynamic_update_slice(
        jnp.zeros((model_width,), jnp.float32), d_floor.reshape(-1), (part_index * local_width,)
    )
    reduced_small = small_sum(jnp.stack([grad_attn, floor_vector, grad_mlp]))
    return (
        layer_out,
        grad_tokens,
        reduced_small[0],
        reduced_small[1],
        attn_red[:, 0 * local_width : 1 * local_width],
        attn_red[:, 1 * local_width : 2 * local_width],
        attn_red[:, 2 * local_width : 3 * local_width],
        attn_red[:, 3 * local_width : 4 * local_width],
        attn_red[:, 4 * local_width : 5 * local_width].T,
        reduced_small[2],
        mlp_red[:, 0:hidden_width],
        mlp_red[:, hidden_width : 2 * hidden_width],
        mlp_red[:, 2 * hidden_width : 3 * hidden_width].T,
    )


def solution(mesh):
    return jax.shard_map(
        shards,
        mesh=mesh,
        in_specs=(
            P("dp", "tensor", None, None),
            P("dp", None, None),
            P(("dp", "tensor")),
            P(("dp", "tensor")),
            P("dp", "tensor"),
            P("dp", "tensor"),
            P("dp", "tensor"),
            P("dp", "tensor"),
            P("tensor", "dp"),
            P(("dp", "tensor")),
            P("dp", "tensor"),
            P("dp", "tensor"),
            P("tensor", "dp"),
            P("dp", "tensor", None, None),
        ),
        out_specs=(
            P("dp", "tensor", None, None),
            P("dp", "tensor", None, None),
            P(("dp", "tensor")),
            P(("dp", "tensor")),
            P("dp", "tensor"),
            P("dp", "tensor"),
            P("dp", "tensor"),
            P("dp", "tensor"),
            P("tensor", "dp"),
            P(("dp", "tensor")),
            P("dp", "tensor"),
            P("dp", "tensor"),
            P("tensor", "dp"),
        ),
        check_vma=False,
    )
```

profile of v0, /device:TPU:0, one launch (start us, length us, event | category | flops | bytes accessed | tf_op | source)
XLA Modules:
  0.0 807.6 jit_solution(461497468060412222)
XLA Ops:
  15.1 11.1 %all-to-all-start = ((f32[128,3,16]{2,1,0:T(4,128)}), f32[128,3,16]{2,1,0:T(4,128)S(1)}, u32[]{:S(2)}, u32[]{:S(2)}) async-start(f32[128,3,16]{2,1,0:T(4,128)} %broadcast_in_dim.29), calls=%async_computation | async-start | bytes 524288 | tf_op jit(solution)/shard_map/all_to_all | solution.py:85
  27.1 11.5 %all-to-all-done = f32[128,3,16]{2,1,0:T(4,128)S(1)} async-done(((f32[128,3,16]{2,1,0:T(4,128)}), f32[128,3,16]{2,1,0:T(4,128)S(1)}, u32[]{:S(2)}, u32[]{:S(2)}) %all-to-all-start) | async-done | bytes 24608 | tf_op jit(solution)/shard_map/all_to_all | solution.py:85
  40.2 15.4 %collective-permute-done = bf16[128,2048]{1,0:T(8,128)(2,1)S(1)} collective-permute-done((bf16[128,2048]{1,0:T(8,128)(2,1)S(1)}, bf16[128,2048]{1,0:T(8,128)(2,1)S(1)}, u32[]{:S(2)}, u32[]{:S(2)}) %collective-permute-start) | collective-permute-done | bytes 524320 | tf_op jit(solution)/shard_map/ppermute | solution.py:62
  61.4 72.5 %all-gather.3.cloned.1.call-done = bf16[2048,2560]{1,0:T(8,128)(2,1)} async-done(((bf16[64,2560]{1,0:T(8,128)(2,1)}), bf16[2048,2560]{1,0:T(8,128)(2,1)}) %all-gather.3.cloned.1.call-update) | async-done | bytes 10485776 | tf_op jit(solution)/shard_map/all_gather | solution.py:129
  133.9 5.3 slice_bitcast_fusion
  167.5 5.4 fusion.74
  176.4 4.1 collective-permute-done.2
  182.8 26.3 %collective-permute-done.3 = f32[128,2048]{1,0:T(8,128)} collective-permute-done((f32[128,2048]{1,0:T(8,128)S(1)}, f32[128,2048]{1,0:T(8,128)}, u32[]{:S(2)}, u32[]{:S(2)}) %collective-permute-start.3) | collective-permute-done | bytes 1048608 | tf_op jit(solution)/shard_map/ppermute | solution.py:73
  211.9 13.1 %collective-permute-done.8 = bf16[128,2048]{1,0:T(8,128)(2,1)} collective-permute-done((bf16[128,2048]{1,0:T(8,128)(2,1)S(1)}, bf16[128,2048]{1,0:T(8,128)(2,1)}, u32[]{:S(2)}, u32[]{:S(2)}) %collective-permute-start.8) | collective-permute-done | bytes 524320 | tf_op jit(solution)/shard_map/ppermute | solution.py:62
  226.3 20.7 %collective-permute-done.4 = bf16[128,2048]{1,0:T(8,128)(2,1)S(1)} collective-permute-done((bf16[128,2048]{1,0:T(8,128)(2,1)S(1)}, bf16[128,2048]{1,0:T(8,128)(2,1)S(1)}, u32[]{:S(2)}, u32[]{:S(2)}) %collective-permute-start.4) | collective-permute-done | bytes 524320 | tf_op jit(solution)/shard_map/ppermute | solution.py:62
  251.4 63.5 %all-gather.5.cloned.1.call-done = bf16[2048,4224]{1,0:T(8,128)(2,1)} async-done(((bf16[64,4224]{1,0:T(8,128)(2,1)}), bf16[2048,4224]{1,0:T(8,128)(2,1)}) %all-gather.5.cloned.1.call-update) | async-done | bytes 17301520 | tf_op jit(solution)/shard_map/all_gather | solution.py:130
  315.0 7.0 fusion
  327.3 7.3 multiply_convert_fusion.1
  345.1 7.9 pad_maximum_fusion
  353.0 21.9 %copy.106 = bf16[2048,4224]{1,0:T(8,128)(2,1)} copy(bf16[2048,4224]{0,1:T(8,128)(2,1)} %pad_maximum_fusion) | data formatting | bytes 34603008
  374.9 6.0 fusion.4
  381.0 5.6 fusion.12
  387.9 5.5 fusion.2
  398.6 29.0 %collective-permute-done.11 = f32[128,2048]{1,0:T(8,128)S(1)} collective-permute-done((f32[128,2048]{1,0:T(8,128)S(1)}, f32[128,2048]{1,0:T(8,128)S(1)}, u32[]{:S(2)}, u32[]{:S(2)}) %collective-permute-start.11) | collective-permute-done | bytes 1048608 | tf_op jit(solution)/shard_map/ppermute | solution.py:73
  428.1 29.3 %collective-permute-done.7 = f32[128,2048]{1,0:T(8,128)S(1)} collective-permute-done((f32[128,2048]{1,0:T(8,128)S(1)}, f32[128,2048]{1,0:T(8,128)S(1)}, u32[]{:S(2)}, u32[]{:S(2)}) %collective-permute-start.7) | collective-permute-done | bytes 1048608 | tf_op jit(solution)/shard_map/ppermute | solution.py:73
  459.6 17.0 %collective-permute-done.12 = bf16[128,2048]{1,0:T(8,128)(2,1)S(1)} collective-permute-done((bf16[128,2048]{1,0:T(8,128)(2,1)S(1)}, bf16[128,2048]{1,0:T(8,128)(2,1)S(1)}, u32[]{:S(2)}, u32[]{:S(2)}) %collective-permute-start.12) | collective-permute-done | bytes 524320 | tf_op jit(solution)/shard_map/ppermute | solution.py:62
  480.0 4.7 fusion.76
  510.0 4.2 fusion.19
  518.6 4.4 fusion.18
  528.4 21.0 %collective-permute-done.15 = f32[128,2048]{1,0:T(8,128)} collective-permute-done((f32[128,2048]{1,0:T(8,128)S(1)}, f32[128,2048]{1,0:T(8,128)}, u32[]{:S(2)}, u32[]{:S(2)}) %collective-permute-start.15) | collective-permute-done | bytes 1048608 | tf_op jit(solution)/shard_map/ppermute | solution.py:73
  552.6 7.2 all-to-all-start.1
  559.8 4.2 fusion.15
  564.0 13.9 %copy.92 = bf16[2048,2560]{1,0:T(8,128)(2,1)} copy(bf16[2048,2560]{0,1:T(8,128)(2,1)} %fusion.15) | data formatting | bytes 20971520 | tf_op jit(solution)/shard_map/concatenate | solution.py:206
  578.0 9.8 %all-to-all-start.2 = ((bf16[32,64,2560]{2,1,0:T(8,128)(2,1)}), bf16[32,64,2560]{2,1,0:T(8,128)(2,1)}, u32[]{:S(2)}, u32[]{:S(2)}) async-start(bf16[32,64,2560]{2,1,0:T(8,128)(2,1)} %bitcast.265), calls=%async_computation.2 | async-start | bytes 20971520 | tf_op jit(solution)/shard_map/all_to_all | solution.py:78
  589.7 163.9 %all-to-all-done.2 = bf16[32,64,2560]{2,1,0:T(8,128)(2,1)} async-done(((bf16[32,64,2560]{2,1,0:T(8,128)(2,1)}), bf16[32,64,2560]{2,1,0:T(8,128)(2,1)}, u32[]{:S(2)}, u32[]{:S(2)}) %all-to-all-start.2) | async-done | bytes 10485792 | tf_op jit(solution)/shard_map/all_to_all | solution.py:78
  753.7 5.8 convert_reduce_fusion
  760.3 31.9 %reduce-scatter.4.cloned.1.call-done = bf16[64,4224]{1,0:T(8,128)(2,1)} async-done(((bf16[2048,4224]{1,0:T(8,128)(2,1)}), bf16[64,4224]{1,0:T(8,128)(2,1)}) %reduce-scatter.4.cloned.1.call-update) | async-done | bytes 540688
  (226 shorter events, 135.8 us)
Async XLA Ops:
  7.2 48.7 %copy-start = (s32[1,4,128]{2,1,0:T(4,128)S(1)}, s32[1,4,128]{2,1,0:T(4,128)}, u32[]{:S(2)}) copy-start(s32[1,4,128]{2,1,0:T(4,128)} %param.16) | copy-start | bytes 6148
  7.2 19.1 %copy-start.3 = (bf16[1,1,128,2048]{3,2,1,0:T(8,128)(2,1)S(1)}, bf16[1,1,128,2048]{3,2,1,0:T(8,128)(2,1)}, u32[]{:S(2)}) copy-start(bf16[1,1,128,2048]{3,2,1,0:T(8,128)(2,1)} %param.15) | copy-start | bytes 1572868
  7.2 126.6 %all-gather.3.cloned.1.call-start = ((), (), s32[]{:S(2)}) async-start(), calls=%async_computation.4 | async-start | bytes 10813440 | tf_op jit(solution)/shard_map/all_gather | solution.py:129
  12.3 302.7 %all-gather.5.cloned.1.call-start = ((), (), s32[]{:S(2)}) async-start(), calls=%async_computation.5 | async-start | bytes 17842176 | tf_op jit(solution)/shard_map/all_gather | solution.py:130
  15.1 23.4 %all-to-all-start = ((f32[128,3,16]{2,1,0:T(4,128)}), f32[128,3,16]{2,1,0:T(4,128)S(1)}, u32[]{:S(2)}, u32[]{:S(2)}) async-start(f32[128,3,16]{2,1,0:T(4,128)} %broadcast_in_dim.29), calls=%async_computation | async-start | bytes 524288 | tf_op jit(solution)/shard_map/all_to_all | solution.py:85
  26.3 765.9 %reduce-scatter.4.cloned.1.call-start = ((), (), s32[]{:S(2)}) async-start(), calls=%async_computation.6 | async-start | bytes 17842176
  27.1 28.7 %copy-start.29 = (f32[128]{0:T(128)}, f32[128]{0:T(128)S(1)}, u32[]{:S(2)}) copy-start(f32[128]{0:T(128)S(1)} %get-tuple-element.105) | copy-start | bytes 1540
  39.2 16.6 %copy-start.27 = (f32[2048]{0:T(1024)}, f32[2048]{0:T(1024)S(1)}, u32[]{:S(2)}) copy-start(f32[2048]{0:T(1024)S(1)} %mul.250) | copy-start | bytes 24580
  39.2 16.7 %copy-start.35 = (s32[4]{0:T(128)S(1)}, s32[4]{0:T(128)}, u32[]{:S(2)}) copy-start(s32[4]{0:T(128)} %constant.52.clone) | copy-start | bytes 52
  39.4 16.3 %collective-permute-start = (bf16[128,2048]{1,0:T(8,128)(2,1)S(1)}, bf16[128,2048]{1,0:T(8,128)(2,1)S(1)}, u32[]{:S(2)}, u32[]{:S(2)}) collective-permute-start(bf16[128,2048]{1,0:T(8,128)(2,1)S(1)} %fusion.62), channel_id=1, source_target_pairs={{0,2},{2,0},{1,3},{3,1},{4,6},{6,4},{5,7},{7,5},{8,10},{10,8},{9,1... | collective-permute-start | bytes 1572872 | tf_op jit(solution)/shard_map/ppermute | solution.py:62
  55.8 2.9 collective-permute-start.1
  176.3 4.2 collective-permute-start.2
  180.7 28.5 %collective-permute-start.3 = (f32[128,2048]{1,0:T(8,128)S(1)}, f32[128,2048]{1,0:T(8,128)}, u32[]{:S(2)}, u32[]{:S(2)}) collective-permute-start(f32[128,2048]{1,0:T(8,128)S(1)} %fusion.88), channel_id=1, source_target_pairs={{0,2},{2,0},{1,3},{3,1},{4,6},{6,4},{5,7},{7,5},{8,10},{10,8},{9,1... | collective-permute-start | bytes 3145736 | tf_op jit(solution)/shard_map/ppermute | solution.py:73
  181.9 43.1 %collective-permute-start.8 = (bf16[128,2048]{1,0:T(8,128)(2,1)S(1)}, bf16[128,2048]{1,0:T(8,128)(2,1)}, u32[]{:S(2)}, u32[]{:S(2)}) collective-permute-start(bf16[128,2048]{1,0:T(8,128)(2,1)S(1)} %bitcast.268), channel_id=1, source_target_pairs={{0,2},{2,0},{1,3},{3,1},{4,6},{6,4},{5,7},{7,5},{8,10},{10,8},{9,1... | collective-permute-start | bytes 1572872 | tf_op jit(solution)/shard_map/ppermute | solution.py:62
  211.6 35.5 %collective-permute-start.4 = (bf16[128,2048]{1,0:T(8,128)(2,1)S(1)}, bf16[128,2048]{1,0:T(8,128)(2,1)S(1)}, u32[]{:S(2)}, u32[]{:S(2)}) collective-permute-start(bf16[128,2048]{1,0:T(8,128)(2,1)S(1)} %multiply_convert_fusion.4), channel_id=1, source_target_pairs={{0,2},{2,0},{1,3},{3,1},{4,6},{6,4},{5,7},{7,5},{8,10},{10,8},{9,1... | collective-permute-start | bytes 1572872 | tf_op jit(solution)/shard_map/ppermute | solution.py:62
  226.1 21.1 %collective-permute-start.9 = (bf16[2,128,2048]{2,1,0:T(8,128)(2,1)S(1)}, bf16[2,128,2048]{2,1,0:T(8,128)(2,1)S(1)}, u32[]{:S(2)}, u32[]{:S(2)}) collective-permute-start(bf16[2,128,2048]{2,1,0:T(8,128)(2,1)S(1)} %pad_maximum_fusion.7), channel_id=1, source_target_pairs={{0,1},{1,0},{2,3},{3,2},{4,5},{5,4},{6,7},{7,6},{8,9},{9,8},{10,11... | collective-permute-start | bytes 3145736 | tf_op jit(solution)/shard_map/ppermute | solution.py:64
  247.1 2.7 collective-permute-start.5
  386.8 6.9 collective-permute-start.10
  393.6 4.2 collective-permute-start.6
  393.8 33.8 %collective-permute-start.11 = (f32[128,2048]{1,0:T(8,128)S(1)}, f32[128,2048]{1,0:T(8,128)S(1)}, u32[]{:S(2)}, u32[]{:S(2)}) collective-permute-start(f32[128,2048]{1,0:T(8,128)S(1)} %fusion.80), channel_id=1, source_target_pairs={{0,2},{2,0},{1,3},{3,1},{4,6},{6,4},{5,7},{7,5},{8,10},{10,8},{9,1... | collective-permute-start | bytes 3145736 | tf_op jit(solution)/shard_map/ppermute | solution.py:73
  398.0 59.4 %collective-permute-start.7 = (f32[128,2048]{1,0:T(8,128)S(1)}, f32[128,2048]{1,0:T(8,128)S(1)}, u32[]{:S(2)}, u32[]{:S(2)}) collective-permute-start(f32[128,2048]{1,0:T(8,128)S(1)} %fusion.83), channel_id=1, source_target_pairs={{0,2},{2,0},{1,3},{3,1},{4,6},{6,4},{5,7},{7,5},{8,10},{10,8},{9,1... | collective-permute-start | bytes 3145736 | tf_op jit(solution)/shard_map/ppermute | solution.py:73
  459.1 17.6 %collective-permute-start.12 = (bf16[128,2048]{1,0:T(8,128)(2,1)S(1)}, bf16[128,2048]{1,0:T(8,128)(2,1)S(1)}, u32[]{:S(2)}, u32[]{:S(2)}) collective-permute-start(bf16[128,2048]{1,0:T(8,128)(2,1)S(1)} %get-tuple-element.75), channel_id=1, source_target_pairs={{0,2},{2,0},{1,3},{3,1},{4,6},{6,4},{5,7},{7,5},{8,10},{10,8},{9,1... | collective-permute-start | bytes 1572872 | tf_op jit(solution)/shard_map/ppermute | solution.py:62
  476.8 3.0 collective-permute-start.13
  509.9 4.5 collective-permute-start.14
  516.1 33.3 %collective-permute-start.15 = (f32[128,2048]{1,0:T(8,128)S(1)}, f32[128,2048]{1,0:T(8,128)}, u32[]{:S(2)}, u32[]{:S(2)}) collective-permute-start(f32[128,2048]{1,0:T(8,128)S(1)} %fusion.77), channel_id=1, source_target_pairs={{0,2},{2,0},{1,3},{3,1},{4,6},{6,4},{5,7},{7,5},{8,10},{10,8},{9,1... | collective-permute-start | bytes 3145736 | tf_op jit(solution)/shard_map/ppermute | solution.py:73
  525.7 23.7 %copy-start.28 = (f32[2048]{0:T(1024)S(1)}, f32[2048]{0:T(1024)}, u32[]{:S(2)}) copy-start(f32[2048]{0:T(1024)} %copy-done.27) | copy-start | bytes 24580
  525.7 23.7 %copy-start.30 = (f32[128]{0:T(128)S(1)}, f32[128]{0:T(128)}, u32[]{:S(2)}) copy-start(f32[128]{0:T(128)} %copy-done.29) | copy-start | bytes 1540
  528.4 31.4 %copy-start.23 = (bf16[512,512]{1,0:T(8,128)(2,1)S(1)}, bf16[512,512]{1,0:T(8,128)(2,1)}, u32[]{:S(2)}) copy-start(bf16[512,512]{1,0:T(8,128)(2,1)} %copy-done.22) | copy-start | bytes 1572868
  552.6 25.4 %all-to-all-start.1 = ((f32[128,3,16]{2,1,0:T(4,128)}), f32[128,3,16]{2,1,0:T(4,128)S(1)}, u32[]{:S(2)}, u32[]{:S(2)}) async-start(f32[128,3,16]{2,1,0:T(4,128)} %copy.91), calls=%async_computation.1 | async-start | bytes 524288 | tf_op jit(solution)/shard_map/all_to_all | solution.py:92
  577.9 9.8 %copy-start.10 = (f32[128,2048]{1,0:T(8,128)S(1)}, f32[128,2048]{1,0:T(8,128)}, u32[]{:S(2)}) copy-start(f32[128,2048]{1,0:T(8,128)} %get-tuple-element.76) | copy-start | bytes 3145732
  578.0 9.8 %copy-start.31 = (f32[128]{0:T(128)S(1)}, f32[128]{0:T(128)}, u32[]{:S(2)}) copy-start(f32[128]{0:T(128)} %get-tuple-element.104) | copy-start | bytes 1540
  578.0 175.7 %all-to-all-start.2 = ((bf16[32,64,2560]{2,1,0:T(8,128)(2,1)}), bf16[32,64,2560]{2,1,0:T(8,128)(2,1)}, u32[]{:S(2)}, u32[]{:S(2)}) async-start(bf16[32,64,2560]{2,1,0:T(8,128)(2,1)} %bitcast.265), calls=%async_computation.2 | async-start | bytes 20971520 | tf_op jit(solution)/shard_map/all_to_all | solution.py:78
  (36 other events, 150.8 us)
Sparse Core Ops, SparseCore 0:
  12.4 121.4 all-gather.2
  136.9 177.9 all-gather.4
  375.0 417.0 reduce-scatter.3
where the time goes:
time: 813 us; the launch traced here: 808 us
  waiting for transfers between devices  527 us (65%)
  matrix products  108 us (13%)
  local copies, waits for them, and re-layouts  86.1 us (11%)
  other arithmetic  37 us (5%)
  starting transfers between devices  34 us (4%)
  between operations  15.3 us (2%)
    all_to_all x1, waiting for transfers between devices, spread_sum(): got = lax.all_to_all(blocks, axis, 0, 0, tiled=False)  164 us
    ppermute x4, waiting for transfers between devices, row_sum(): return mine + lax.ppermute(theirs, 'tensor', ACROSS)  106 us
    all_gather x1, waiting for transfers between devices, shards(): attn_all = lax.all_gather(attn_pack, 'dp', axis=0, tiled=True)  72.5 us
    ppermute x4, waiting for transfers between devices, row_gather(): across = lax.ppermute(values, 'tensor', ACROSS)  66.2 us
    all_gather x1, waiting for transfers between devices, shards(): mlp_all = lax.all_gather(mlp_pack, 'dp', axis=0, tiled=True)  63.5 us
    unnamed x101, local copies, waits for them, and re-layouts  40.4 us
    dot_general x8, matrix products, matmul_plain(): return jnp.dot(left, right, preferred_element_type=jnp.float32)  36.9 us
    unnamed x4, waiting for transfers between devices  31.9 us
  transfers between devices with their start and end apart: 22, of which 19 were waited for; matrix products, arithmetic and copies ran while one was open for 19% of the time, Pallas kernels for 0%

commit v1 on v0

--- a/solution.py
+++ b/solution.py
@@ -1,3 +1,4 @@
+import functools
 import jax
 import jax.numpy as jnp
 from jax import lax
@@ -6,6 +7,21 @@
 HK = 128
 HIGHEST = lax.Precision.HIGHEST
 epsilon = 1e-06
+
+
+def _push_stops_all(my_tile, mesh_dim):
+    return jnp.concatenate(
+        lax.all_to_all(
+            jnp.stack(tuple((my_tile for _ in range(lax.axis_size(mesh_dim)))), axis=0),
+            axis_name=mesh_dim,
+            split_axis=0,
+            concat_axis=0,
+        ),
+        axis=0,
+    )
+
+
+try_all_yards = functools.partial(_push_stops_all, mesh_dim="dp")
 
 
 def row_scale(values):
@@ -126,7 +142,7 @@
     cot_local = cotangent[0].reshape(-1, model_width)
     attn_pack = jnp.concatenate([w_query, w_forget, w_value, w_outgate, w_output.T], axis=1)
     mlp_pack = jnp.concatenate([w_gate, w_up, w_down.T], axis=1)
-    attn_all = lax.all_gather(attn_pack, "dp", axis=0, tiled=True)
+    attn_all = try_all_yards(attn_pack)
     mlp_all = lax.all_gather(mlp_pack, "dp", axis=0, tiled=True)
     wq_all = attn_all[:, 0 * local_width : 1 * local_width]
     wf_all = attn_all[:, 1 * local_width : 2 * local_width]

time: 813 us -> 841 us (1.034)
  starting transfers between devices: 34 us -> 57.9 us
    ppermute x4, waiting for transfers between devices: 66.2 us -> 168 us  [row_gather(): across = lax.ppermute(values, 'tensor', ACROSS)]
    all_gather x1 -> x0, waiting for transfers between devices: 72.5 us -> none  [shards(): attn_all = lax.all_gather(attn_pack, 'dp', axis=0, tiled=True)]
    all_gather x1, waiting for transfers between devices: 63.5 us -> 0.01 us  [shards(): mlp_all = lax.all_gather(mlp_pack, 'dp', axis=0, tiled=True)]
    all_to_all x0 -> x1, waiting for transfers between devices: none -> 34.5 us  [_push_stops_all(): lax.all_to_all(jnp.stack(tuple((my_tile for _ in range(lax.axis_size(mesh...]
    all_to_all x1, starting transfers between devices: 7.17 us -> 23.6 us  [small_sum(): lax.all_to_all(jnp.swapaxes(blocks, 0, 1), ('dp', 'tensor'), 0, 0, tiled=...]
    unnamed x101 -> x97, local copies, waits for them, and re-layouts: 40.4 us -> 33.8 us
    unnamed x4 -> x3, waiting for transfers between devices: 31.9 us -> 33.2 us
  transfers between devices with their start and end apart: 22 -> 22, of which waited for: 19 -> 17; matrix products, arithmetic and copies ran while one was open for 19% -> 20% of each run, Pallas kernels for 0% -> 0%
where the time goes in v1:
time: 841 us; the launch traced here: 835 us
  waiting for transfers between devices  525 us (62%)
  matrix products  115 us (14%)
  local copies, waits for them, and re-layouts  83.8 us (10%)
  starting transfers between devices  57.9 us (7%)
  other arithmetic  37.9 us (5%)
  between operations  15.6 us (2%)
    ppermute x4, waiting for transfers between devices, row_gather(): across = lax.ppermute(values, 'tensor', ACROSS)  168 us
    all_to_all x1, waiting for transfers between devices, spread_sum(): got = lax.all_to_all(blocks, axis, 0, 0, tiled=False)  160 us
    ppermute x4, waiting for transfers between devices, row_sum(): return mine + lax.ppermute(theirs, 'tensor', ACROSS)  108 us
    dot_general x8, matrix products, matmul_plain(): return jnp.dot(left, right, preferred_element_type=jnp.float32)  36.4 us
    all_to_all x1, waiting for transfers between devices, _push_stops_all(): lax.all_to_all(jnp.stack(tuple((my_tile for _ in range(lax.axis_size(mesh...  34.5 us
    unnamed x97, local copies, waits for them, and re-layouts  33.8 us
    unnamed x3, waiting for transfers between devices  33.2 us
    dot_general x8, matrix products, times_trans(): lax.dot_general(left, right, (((1,), (1,)), ((), ())), preferred_element_...  32.2 us
  transfers between devices with their start and end apart: 22, of which 17 were waited for; matrix products, arithmetic and copies ran while one was open for 20% of the time, Pallas kernels for 0%

profile of v1, /device:TPU:0, one launch (start us, length us, event | category | flops | bytes accessed | tf_op | source)
XLA Modules:
  0.0 834.8 jit_solution(5852013289236495500)
XLA Ops:
  10.8 11.1 %all-to-all-start = ((f32[128,3,16]{2,1,0:T(4,128)}), f32[128,3,16]{2,1,0:T(4,128)S(1)}, u32[]{:S(2)}, u32[]{:S(2)}) async-start(f32[128,3,16]{2,1,0:T(4,128)} %broadcast_in_dim.29), calls=%async_computation | async-start | bytes 524288 | tf_op jit(solution)/shard_map/all_to_all | solution.py:101
  22.1 10.7 %all-to-all-done = f32[128,3,16]{2,1,0:T(4,128)S(1)} async-done(((f32[128,3,16]{2,1,0:T(4,128)}), f32[128,3,16]{2,1,0:T(4,128)S(1)}, u32[]{:S(2)}, u32[]{:S(2)}) %all-to-all-start) | async-done | bytes 24608 | tf_op jit(solution)/shard_map/all_to_all | solution.py:101
  32.8 5.2 stack.44
  38.0 5.2 all-to-all-start.1
  45.6 134.0 %collective-permute-done = bf16[128,2048]{1,0:T(8,128)(2,1)S(1)} collective-permute-done((bf16[128,2048]{1,0:T(8,128)(2,1)S(1)}, bf16[128,2048]{1,0:T(8,128)(2,1)S(1)}, u32[]{:S(2)}, u32[]{:S(2)}) %collective-permute-start) | collective-permute-done | bytes 524320 | tf_op jit(solution)/shard_map/ppermute | solution.py:78
  185.4 34.5 %all-to-all-done.1 = bf16[32,64,2560]{2,1,0:T(8,128)(2,1)} async-done(((bf16[32,64,2560]{2,1,0:T(8,128)(2,1)}), bf16[32,64,2560]{2,1,0:T(8,128)(2,1)}, u32[]{:S(2)}, u32[]{:S(2)}) %all-to-all-start.1) | async-done | bytes 10485792 | tf_op jit(solution)/shard_map/all_to_all | solution.py:14
  219.9 5.4 slice_bitcast_fusion
  253.5 4.9 fusion.74
  270.6 24.6 %collective-permute-done.3 = f32[128,2048]{1,0:T(8,128)} collective-permute-done((f32[128,2048]{1,0:T(8,128)S(1)}, f32[128,2048]{1,0:T(8,128)}, u32[]{:S(2)}, u32[]{:S(2)}) %collective-permute-start.3) | collective-permute-done | bytes 1048608 | tf_op jit(solution)/shard_map/ppermute | solution.py:89
  298.1 8.2 collective-permute-done.8
  307.8 9.6 %collective-permute-done.4 = bf16[128,2048]{1,0:T(8,128)(2,1)S(1)} collective-permute-done((bf16[128,2048]{1,0:T(8,128)(2,1)S(1)}, bf16[128,2048]{1,0:T(8,128)(2,1)S(1)}, u32[]{:S(2)}, u32[]{:S(2)}) %collective-permute-start.4) | collective-permute-done | bytes 524320 | tf_op jit(solution)/shard_map/ppermute | solution.py:78
  321.8 7.0 fusion
  334.1 7.3 multiply_convert_fusion.1
  351.9 7.8 pad_maximum_fusion
  359.7 21.0 %copy.104 = bf16[2048,4224]{1,0:T(8,128)(2,1)} copy(bf16[2048,4224]{0,1:T(8,128)(2,1)} %pad_maximum_fusion) | data formatting | bytes 34603008
  380.8 6.0 fusion.4
  386.8 5.5 fusion.12
  393.7 5.5 fusion.2
  404.2 29.6 %collective-permute-done.11 = f32[128,2048]{1,0:T(8,128)S(1)} collective-permute-done((f32[128,2048]{1,0:T(8,128)S(1)}, f32[128,2048]{1,0:T(8,128)S(1)}, u32[]{:S(2)}, u32[]{:S(2)}) %collective-permute-start.11) | collective-permute-done | bytes 1048608 | tf_op jit(solution)/shard_map/ppermute | solution.py:89
  434.3 28.8 %collective-permute-done.7 = f32[128,2048]{1,0:T(8,128)S(1)} collective-permute-done((f32[128,2048]{1,0:T(8,128)S(1)}, f32[128,2048]{1,0:T(8,128)S(1)}, u32[]{:S(2)}, u32[]{:S(2)}) %collective-permute-start.7) | collective-permute-done | bytes 1048608 | tf_op jit(solution)/shard_map/ppermute | solution.py:89
  464.8 16.0 %collective-permute-done.12 = bf16[128,2048]{1,0:T(8,128)(2,1)S(1)} collective-permute-done((bf16[128,2048]{1,0:T(8,128)(2,1)S(1)}, bf16[128,2048]{1,0:T(8,128)(2,1)S(1)}, u32[]{:S(2)}, u32[]{:S(2)}) %collective-permute-start.12) | collective-permute-done | bytes 524320 | tf_op jit(solution)/shard_map/ppermute | solution.py:78
  484.0 4.7 fusion.76
  520.9 4.3 fusion.19
  528.5 4.4 fusion.18
  538.3 24.5 %collective-permute-done.15 = f32[128,2048]{1,0:T(8,128)} collective-permute-done((f32[128,2048]{1,0:T(8,128)S(1)}, f32[128,2048]{1,0:T(8,128)}, u32[]{:S(2)}, u32[]{:S(2)}) %collective-permute-start.15) | collective-permute-done | bytes 1048608 | tf_op jit(solution)/shard_map/ppermute | solution.py:89
  566.1 23.6 %all-to-all-start.2 = ((f32[128,3,16]{2,1,0:T(4,128)}), f32[128,3,16]{2,1,0:T(4,128)S(1)}, u32[]{:S(2)}, u32[]{:S(2)}) async-start(f32[128,3,16]{2,1,0:T(4,128)} %copy.89), calls=%async_computation.2 | async-start | bytes 524288 | tf_op jit(solution)/shard_map/all_to_all | solution.py:108
  589.7 4.2 fusion.15
  593.9 13.8 %copy.90 = bf16[2048,2560]{1,0:T(8,128)(2,1)} copy(bf16[2048,2560]{0,1:T(8,128)(2,1)} %fusion.15) | data formatting | bytes 20971520 | tf_op jit(solution)/shard_map/concatenate | solution.py:222
  607.7 9.7 %all-to-all-start.3 = ((bf16[32,64,2560]{2,1,0:T(8,128)(2,1)}), bf16[32,64,2560]{2,1,0:T(8,128)(2,1)}, u32[]{:S(2)}, u32[]{:S(2)}) async-start(bf16[32,64,2560]{2,1,0:T(8,128)(2,1)} %bitcast.266), calls=%async_computation.3 | async-start | bytes 20971520 | tf_op jit(solution)/shard_map/all_to_all | solution.py:94
  619.4 159.8 %all-to-all-done.3 = bf16[32,64,2560]{2,1,0:T(8,128)(2,1)} async-done(((bf16[32,64,2560]{2,1,0:T(8,128)(2,1)}), bf16[32,64,2560]{2,1,0:T(8,128)(2,1)}, u32[]{:S(2)}, u32[]{:S(2)}) %all-to-all-start.3) | async-done | bytes 10485792 | tf_op jit(solution)/shard_map/all_to_all | solution.py:94
  779.2 5.8 convert_reduce_fusion
  785.9 33.1 %reduce-scatter.4.cloned.1.call-done = bf16[64,4224]{1,0:T(8,128)(2,1)} async-done(((bf16[2048,4224]{1,0:T(8,128)(2,1)}), bf16[64,4224]{1,0:T(8,128)(2,1)}) %reduce-scatter.4.cloned.1.call-update) | async-done | bytes 540688
  (221 shorter events, 143.3 us)
Async XLA Ops:
  7.2 172.7 %copy-start = (s32[1,4,128]{2,1,0:T(4,128)S(1)}, s32[1,4,128]{2,1,0:T(4,128)}, u32[]{:S(2)}) copy-start(s32[1,4,128]{2,1,0:T(4,128)} %param.16) | copy-start | bytes 6148
  7.2 14.8 %copy-start.30 = (bf16[64,512]{1,0:T(8,128)(2,1)S(1)}, bf16[64,512]{1,0:T(8,128)(2,1)}, u32[]{:S(2)}) copy-start(bf16[64,512]{1,0:T(8,128)(2,1)} %param.21) | copy-start | bytes 196612
  7.2 14.8 %copy-start.31 = (bf16[64,512]{1,0:T(8,128)(2,1)S(1)}, bf16[64,512]{1,0:T(8,128)(2,1)}, u32[]{:S(2)}) copy-start(bf16[64,512]{1,0:T(8,128)(2,1)} %param.22) | copy-start | bytes 196612
  7.2 14.8 %copy-start.32 = (bf16[512,64]{0,1:T(8,128)(2,1)S(1)}, bf16[512,64]{0,1:T(8,128)(2,1)}, u32[]{:S(2)}) copy-start(bf16[512,64]{0,1:T(8,128)(2,1)} %param.23) | copy-start | bytes 196612
  7.2 314.5 %all-gather.2.cloned.1.call-start = ((), (), s32[]{:S(2)}) async-start(), calls=%async_computation.5 | async-start | bytes 17842176 | tf_op jit(solution)/shard_map/all_gather | solution.py:146
  10.8 22.0 %all-to-all-start = ((f32[128,3,16]{2,1,0:T(4,128)}), f32[128,3,16]{2,1,0:T(4,128)S(1)}, u32[]{:S(2)}, u32[]{:S(2)}) async-start(f32[128,3,16]{2,1,0:T(4,128)} %broadcast_in_dim.29), calls=%async_computation | async-start | bytes 524288 | tf_op jit(solution)/shard_map/all_to_all | solution.py:101
  38.0 181.9 %all-to-all-start.1 = ((bf16[32,64,2560]{2,1,0:T(8,128)(2,1)}), bf16[32,64,2560]{2,1,0:T(8,128)(2,1)}, u32[]{:S(2)}, u32[]{:S(2)}) async-start(bf16[32,64,2560]{2,1,0:T(8,128)(2,1)} %stack.44), calls=%async_computation.1 | async-start | bytes 20971520 | tf_op jit(solution)/shard_map/all_to_all | solution.py:14
  43.2 775.9 %reduce-scatter.4.cloned.1.call-start = ((), (), s32[]{:S(2)}) async-start(), calls=%async_computation.6 | async-start | bytes 17842176
  43.9 135.7 %copy-start.33 = (f32[128]{0:T(128)}, f32[128]{0:T(128)S(1)}, u32[]{:S(2)}) copy-start(f32[128]{0:T(128)S(1)} %get-tuple-element.105) | copy-start | bytes 1540
  44.6 135.1 %copy-start.26 = (f32[2048]{0:T(1024)}, f32[2048]{0:T(1024)S(1)}, u32[]{:S(2)}) copy-start(f32[2048]{0:T(1024)S(1)} %mul.250) | copy-start | bytes 24580
  44.6 135.2 %copy-start.36 = (s32[4]{0:T(128)S(1)}, s32[4]{0:T(128)}, u32[]{:S(2)}) copy-start(s32[4]{0:T(128)} %constant.52.clone) | copy-start | bytes 52
  44.8 134.8 %collective-permute-start = (bf16[128,2048]{1,0:T(8,128)(2,1)S(1)}, bf16[128,2048]{1,0:T(8,128)(2,1)S(1)}, u32[]{:S(2)}, u32[]{:S(2)}) collective-permute-start(bf16[128,2048]{1,0:T(8,128)(2,1)S(1)} %fusion.62), channel_id=1, source_target_pairs={{0,2},{2,0},{1,3},{3,1},{4,6},{6,4},{5,7},{7,5},{8,10},{10,8},{9,1... | collective-permute-start | bytes 1572872 | tf_op jit(solution)/shard_map/ppermute | solution.py:78
  179.7 2.9 collective-permute-start.1
  261.7 4.2 collective-permute-start.2
  266.1 29.0 %collective-permute-start.3 = (f32[128,2048]{1,0:T(8,128)S(1)}, f32[128,2048]{1,0:T(8,128)}, u32[]{:S(2)}, u32[]{:S(2)}) collective-permute-start(f32[128,2048]{1,0:T(8,128)S(1)} %fusion.88), channel_id=1, source_target_pairs={{0,2},{2,0},{1,3},{3,1},{4,6},{6,4},{5,7},{7,5},{8,10},{10,8},{9,1... | collective-permute-start | bytes 3145736 | tf_op jit(solution)/shard_map/ppermute | solution.py:89
  269.4 37.0 %collective-permute-start.8 = (bf16[128,2048]{1,0:T(8,128)(2,1)S(1)}, bf16[128,2048]{1,0:T(8,128)(2,1)}, u32[]{:S(2)}, u32[]{:S(2)}) collective-permute-start(bf16[128,2048]{1,0:T(8,128)(2,1)S(1)} %bitcast.267), channel_id=1, source_target_pairs={{0,2},{2,0},{1,3},{3,1},{4,6},{6,4},{5,7},{7,5},{8,10},{10,8},{9,1... | collective-permute-start | bytes 1572872 | tf_op jit(solution)/shard_map/ppermute | solution.py:78
  297.6 19.7 %collective-permute-start.4 = (bf16[128,2048]{1,0:T(8,128)(2,1)S(1)}, bf16[128,2048]{1,0:T(8,128)(2,1)S(1)}, u32[]{:S(2)}, u32[]{:S(2)}) collective-permute-start(bf16[128,2048]{1,0:T(8,128)(2,1)S(1)} %multiply_convert_fusion.4), channel_id=1, source_target_pairs={{0,2},{2,0},{1,3},{3,1},{4,6},{6,4},{5,7},{7,5},{8,10},{10,8},{9,1... | collective-permute-start | bytes 1572872 | tf_op jit(solution)/shard_map/ppermute | solution.py:78
  307.5 10.0 %collective-permute-start.9 = (bf16[2,128,2048]{2,1,0:T(8,128)(2,1)S(1)}, bf16[2,128,2048]{2,1,0:T(8,128)(2,1)S(1)}, u32[]{:S(2)}, u32[]{:S(2)}) collective-permute-start(bf16[2,128,2048]{2,1,0:T(8,128)(2,1)S(1)} %pad_maximum_fusion.7), channel_id=1, source_target_pairs={{0,1},{1,0},{2,3},{3,2},{4,5},{5,4},{6,7},{7,6},{8,9},{9,8},{10,11... | collective-permute-start | bytes 3145736 | tf_op jit(solution)/shard_map/ppermute | solution.py:80
  317.4 2.7 collective-permute-start.5
  392.6 7.3 collective-permute-start.10
  399.4 4.3 collective-permute-start.6
  400.0 33.8 %collective-permute-start.11 = (f32[128,2048]{1,0:T(8,128)S(1)}, f32[128,2048]{1,0:T(8,128)S(1)}, u32[]{:S(2)}, u32[]{:S(2)}) collective-permute-start(f32[128,2048]{1,0:T(8,128)S(1)} %fusion.80), channel_id=1, source_target_pairs={{0,2},{2,0},{1,3},{3,1},{4,6},{6,4},{5,7},{7,5},{8,10},{10,8},{9,1... | collective-permute-start | bytes 3145736 | tf_op jit(solution)/shard_map/ppermute | solution.py:89
  403.8 59.3 %collective-permute-start.7 = (f32[128,2048]{1,0:T(8,128)S(1)}, f32[128,2048]{1,0:T(8,128)S(1)}, u32[]{:S(2)}, u32[]{:S(2)}) collective-permute-start(f32[128,2048]{1,0:T(8,128)S(1)} %fusion.83), channel_id=1, source_target_pairs={{0,2},{2,0},{1,3},{3,1},{4,6},{6,4},{5,7},{7,5},{8,10},{10,8},{9,1... | collective-permute-start | bytes 3145736 | tf_op jit(solution)/shard_map/ppermute | solution.py:89
  464.8 16.0 %collective-permute-start.12 = (bf16[128,2048]{1,0:T(8,128)(2,1)S(1)}, bf16[128,2048]{1,0:T(8,128)(2,1)S(1)}, u32[]{:S(2)}, u32[]{:S(2)}) collective-permute-start(bf16[128,2048]{1,0:T(8,128)(2,1)S(1)} %get-tuple-element.75), channel_id=1, source_target_pairs={{0,2},{2,0},{1,3},{3,1},{4,6},{6,4},{5,7},{7,5},{8,10},{10,8},{9,1... | collective-permute-start | bytes 1572872 | tf_op jit(solution)/shard_map/ppermute | solution.py:78
  480.9 3.0 collective-permute-start.13
  520.7 4.5 collective-permute-start.14
  526.9 35.9 %collective-permute-start.15 = (f32[128,2048]{1,0:T(8,128)S(1)}, f32[128,2048]{1,0:T(8,128)}, u32[]{:S(2)}, u32[]{:S(2)}) collective-permute-start(f32[128,2048]{1,0:T(8,128)S(1)} %fusion.77), channel_id=1, source_target_pairs={{0,2},{2,0},{1,3},{3,1},{4,6},{6,4},{5,7},{7,5},{8,10},{10,8},{9,1... | collective-permute-start | bytes 3145736 | tf_op jit(solution)/shard_map/ppermute | solution.py:89
  535.6 27.3 %copy-start.27 = (f32[2048]{0:T(1024)S(1)}, f32[2048]{0:T(1024)}, u32[]{:S(2)}) copy-start(f32[2048]{0:T(1024)} %copy-done.26) | copy-start | bytes 24580
  535.6 27.3 %copy-start.34 = (f32[128]{0:T(128)S(1)}, f32[128]{0:T(128)}, u32[]{:S(2)}) copy-start(f32[128]{0:T(128)} %copy-done.33) | copy-start | bytes 1540
  538.3 51.4 %copy-start.23 = (bf16[512,512]{1,0:T(8,128)(2,1)S(1)}, bf16[512,512]{1,0:T(8,128)(2,1)}, u32[]{:S(2)}) copy-start(bf16[512,512]{1,0:T(8,128)(2,1)} %copy-done.22) | copy-start | bytes 1572868
  566.1 41.6 %all-to-all-start.2 = ((f32[128,3,16]{2,1,0:T(4,128)}), f32[128,3,16]{2,1,0:T(4,128)S(1)}, u32[]{:S(2)}, u32[]{:S(2)}) async-start(f32[128,3,16]{2,1,0:T(4,128)} %copy.89), calls=%async_computation.2 | async-start | bytes 524288 | tf_op jit(solution)/shard_map/all_to_all | solution.py:108
  607.7 171.5 %all-to-all-start.3 = ((bf16[32,64,2560]{2,1,0:T(8,128)(2,1)}), bf16[32,64,2560]{2,1,0:T(8,128)(2,1)}, u32[]{:S(2)}, u32[]{:S(2)}) async-start(bf16[32,64,2560]{2,1,0:T(8,128)(2,1)} %bitcast.266), calls=%async_computation.3 | async-start | bytes 20971520 | tf_op jit(solution)/shard_map/all_to_all | solution.py:94
  (34 other events, 175.1 us)
Sparse Core Ops, SparseCore 0:
  11.1 288.4 all-gather.1
  380.9 438.1 reduce-scatter.3
